TPU v7x, 32 devices: a whole 2x2x4 slice. The times are simulated.
32 devices in a mesh: vocab: 8 (over z, x), batch: 4 (over y, core).
Axes of the slice: x: 2, y: 2, z: 4, core: 2. Of those that a mesh axis runs over, the one named last changes fastest.
Arguments:
- hidden: bfloat16 [256, 1024], P(('vocab', 'batch'))
- embedding: bfloat16 [8192, 1024], P('vocab')
- block_counts: int32 [64], P('vocab'), may hold values from 1 to 4095
- lang_blocks: int32 [200, 64], replicated, may hold values from -1 to 63, as said below
- sent_lang: int32 [4], replicated, may hold values from 0 to 199
- targets: int32 [256], replicated, may hold values from 0 to 8191, as said below
Outputs:
- token_loss: float32 [256], P(('vocab', 'batch'))
- grad_embed: bfloat16 [8192, 1024], P(('vocab', 'batch'))
Inputs may be any that keep to these rules, and one draw needn't show every extreme that they name: `lang_blocks`: each list holds distinct block numbers and then -1 padding; the first entry of every list is block 0; at least 16 entries are blocks, and some language fills all 64 entries. `targets`: the target of token t lies in a block listed for the language of sentence t // 64.
All inputs are finite; a program needn't handle non-finite values.
Results may differ from a plain program's by a relative error of at most 0.0075.
Values may be sent and summed in bfloat16 or wider, within the bound.
No kernel may reach another device: no remote copies, remote signals or barrier semaphores. Data moves between devices by JAX's collectives and lax.ppermute only.
A program may use at most 64 MiB of HBM per device.

v0:
```python
import jax
import jax.numpy as jnp
from jax import lax
from jax.sharding import PartitionSpec as P

SEQ = 64
masked_fill = -1e30


def body(hidden, embedding, block_counts, lang_blocks, sent_lang, targets):
    tok_dev = hidden.shape[0]
    vocab_count = lax.axis_size("vocab")
    batch_count = lax.axis_size("batch")
    vocab_index = lax.axis_index("vocab")
    batch_index = lax.axis_index("batch")
    local_rows = embedding.shape[0]
    local_blocks = block_counts.shape[0]
    block_width = local_rows // local_blocks
    gathered = lax.all_gather(hidden, "vocab", axis=0, tiled=True)
    token_count = gathered.shape[0]
    token_ids = (
        (jnp.arange(vocab_count, dtype=jnp.int32)[:, None] * batch_count + batch_index) * tok_dev
        + jnp.arange(tok_dev, dtype=jnp.int32)[None, :]
    ).reshape(-1)
    target_ids = lax.dynamic_index_in_dim(
        targets.reshape(vocab_count, batch_count, tok_dev), batch_index, 1, keepdims=False
    ).reshape(-1)
    sentence = token_ids // SEQ
    sentence_hit = sentence[:, None] == jnp.arange(sent_lang.shape[0], dtype=jnp.int32)[None, :]
    token_language = jnp.sum(jnp.where(sentence_hit, sent_lang[None, :], 0), axis=1)
    block_ids = vocab_index * local_blocks + jnp.arange(local_blocks, dtype=jnp.int32)
    member = jnp.any(lang_blocks[:, :, None] == block_ids[None, None, :], axis=1).astype(
        jnp.float32
    )
    language_hit = (
        token_language[:, None] == jnp.arange(lang_blocks.shape[0], dtype=jnp.int32)[None, :]
    ).astype(jnp.float32)
    allowed = jnp.dot(language_hit, member, precision=lax.Precision.HIGHEST) > 0.5
    allowed_cells = allowed[:, :, None]
    raw_scores = lax.dot_general(
        gathered, embedding, (((1,), (1,)), ((), ())), preferred_element_type=jnp.float32
    )
    log_sampling = jnp.log(block_counts.astype(jnp.float32))
    logits = (
        raw_scores.reshape(token_count, local_blocks, block_width) - log_sampling[None, :, None]
    )
    masked = jnp.where(allowed_cells, logits, masked_fill)
    word_ids = (vocab_index * local_rows + jnp.arange(local_rows, dtype=jnp.int32)).reshape(
        local_blocks, block_width
    )
    is_target = word_ids[None, :, :] == target_ids[:, None, None]
    local_peak = jnp.max(masked, axis=(1, 2))
    local_target = jnp.sum(jnp.where(is_target, logits, 0.0), axis=(1, 2))
    peak_value = lax.pmax(local_peak, "vocab")
    local_total = jnp.sum(
        jnp.where(allowed_cells, jnp.exp(masked - peak_value[:, None, None]), 0.0), axis=(1, 2)
    )
    denominator, target_logit = lax.psum((local_total, local_target), "vocab")
    log_total = peak_value + jnp.log(denominator)
    every_loss = log_total - target_logit
    token_loss = lax.dynamic_slice_in_dim(every_loss, vocab_index * tok_dev, tok_dev, 0)
    softmax_weights = jnp.where(allowed_cells, jnp.exp(logits - log_total[:, None, None]), 0.0)
    grad_logits = (
        (softmax_weights - is_target.astype(jnp.float32))
        .astype(jnp.bfloat16)
        .reshape(token_count, local_rows)
    )
    columns = lax.all_to_all(grad_logits, "batch", split_axis=1, concat_axis=0, tiled=True)
    everyone = lax.all_gather(gathered, "batch", axis=0, tiled=True)
    summed = jnp.zeros((columns.shape[1], gathered.shape[1]), jnp.float32)
    for source in range(batch_count):
        slice_grad = columns[source * token_count : (source + 1) * token_count]
        slice_rows = everyone[source * token_count : (source + 1) * token_count]
        contribution = lax.dot_general(
            slice_grad, slice_rows, (((0,), (0,)), ((), ())), preferred_element_type=jnp.float32
        )
        rounded = lax.optimization_barrier(contribution.astype(jnp.bfloat16))
        summed = summed + rounded.astype(jnp.float32)
    grad_embed = summed.astype(jnp.bfloat16)
    return (token_loss, grad_embed)


def solution(mesh):
    in_specs = (P(("vocab", "batch"), None), P("vocab", None), P("vocab"), P(), P(), P())
    out_specs = (P(("vocab", "batch")), P(("vocab", "batch"), None))
    return jax.shard_map(body, mesh=mesh, in_specs=in_specs, out_specs=out_specs, check_vma=False)
```

profile of v0, /device:TPU:0, one launch (start us, length us, event | category | flops | bytes accessed | tf_op | source)
XLA Modules:
  0.0 92.3 jit_solution(3741572874803002125)
XLA Ops:
  0.6 0.0 copy-start
  0.7 0.8 convert_log_fusion
  1.5 0.1 broadcast_bitcast_fusion
  1.6 0.1 iota_add_fusion
  1.6 0.1 add.93
  1.7 1.0 %compare_reduce_fusion = pred[200,8]{0,1:T(8,128)(4,1)S(1)} fusion(s32[200,64]{0,1:T(8,128)} %param.9, s32[8]{0:T(128)S(1)} %iota_add_fusion.1), kind=kLoop, calls=%fused_computation.7 | loop fusion | flops 203200 | bytes 52832 | tf_op jit(solution)/shard_map/reduce_or | solution.py:32
  2.7 0.7 select_reduce_fusion.1
  3.5 0.2 convolution_compare_fusion
  3.7 0.1 copy.13
  3.8 0.8 reshape.91
  4.6 0.1 eq.66
  4.7 32.5 %all_gather.6 = bf16[64,1024]{1,0:T(8,128)(2,1)S(1)} all-gather(bf16[8,1024]{1,0:T(8,128)(2,1)} %param.6), channel_id=1, replica_groups=mesh['vocab'=8,'batch'=4] {'vocab'}, dimensions={0}, use_global_device_ids=true | all-gather | bytes 147456 | tf_op jit(solution)/shard_map/all_gather | solution.py:19
  37.2 0.1 broadcast_in_dim.53
  37.3 0.0 copy-done
  37.3 0.9 fusion.3
  38.2 21.3 %pmax.7 = f32[64]{0:T(128)S(1)} all-reduce(f32[64]{0:T(128)S(1)} %get-tuple-element.8), channel_id=1, replica_groups=mesh['vocab'=8,'batch'=4] {'vocab'}, use_global_device_ids=true, to_apply=%region_3.4 | all-reduce | flops 64 | bytes 512 | tf_op jit(solution)/shard_map/pmax | solution.py:54
  59.5 0.3 fusion
  59.8 17.1 %all-reduce = (f32[64]{0:T(128)S(1)}, f32[64]{0:T(128)S(1)}) all-reduce(f32[64]{0:T(128)S(1)} %get-tuple-element.3, f32[64]{0:T(128)S(1)} %get-tuple-element.2), channel_id=1, replica_groups=mesh['vocab'=8,'batch'=4] {'vocab'}, use_global_device_ids=true, to_apply=%region_5.6 | all-reduce | flops 128 | bytes 1024 | tf_op jit(solution)/shard_map/psum | solution.py:58
  76.9 0.1 fusion.2
  77.1 0.7 copy.21
  77.7 3.3 %all-to-all-start = ((bf16[64,4,256]{2,0,1:T(8,128)(2,1)}), bf16[64,4,256]{2,0,1:T(8,128)(2,1)S(1)}, u32[]{:S(2)}, u32[]{:S(2)}) async-start(bf16[64,4,256]{2,0,1:T(8,128)(2,1)} %bitcast.32), calls=%async_computation | async-start | bytes 262144 | tf_op jit(solution)/shard_map/all_to_all | solution.py:68
  81.1 8.2 %all_gather.7 = bf16[256,1024]{1,0:T(8,128)(2,1)S(1)} all-gather(bf16[64,1024]{1,0:T(8,128)(2,1)S(1)} %all_gather.6), channel_id=1, replica_groups=mesh['vocab'=8,'batch'=4] {'batch'}, dimensions={0}, use_global_device_ids=true | all-gather | bytes 655360 | tf_op jit(solution)/shard_map/all_gather | solution.py:69
  89.3 0.6 dynamic_slice.8
  89.9 0.0 all-to-all-done
  89.9 0.3 convolution_convert_fusion
  90.2 0.3 convolution_convert_fusion.1
  90.5 0.3 convolution_convert_fusion.2
  90.9 0.3 convolution_convert_fusion.3
  91.2 1.1 %add_convert_fusion = bf16[256,1024]{1,0:T(8,128)(2,1)} fusion(bf16[256,1024]{1,0:T(8,128)(2,1)S(1)} %convolution_convert_fusion, bf16[256,1024]{1,0:T(8,128)(2,1)S(1)} %convolution_convert_fusion.1, bf16[256,1024]{1,0:T(8,128)(2,1)S(1)} %convolution_convert_fusion.2, bf16[256,1024]{1,0:T(8,128)(2,1)S(1)} %convolution_convert_fusion.3), kind=kLoop, calls=%fused_computation.6 | loop fusion | flops 2097152 | bytes 2621440 | tf_op jit(solution)/shard_map/convert_element_type | solution.py:79
  (6 shorter events, 0.1 us)
Async XLA Ops:
  0.6 36.7 %copy-start = (bf16[1024,1024]{1,0:T(8,128)(2,1)S(1)}, bf16[1024,1024]{1,0:T(8,128)(2,1)}, u32[]{:S(2)}) copy-start(bf16[1024,1024]{1,0:T(8,128)(2,1)} %param.7) | copy-start | bytes 6291460
  77.7 12.2 %all-to-all-start = ((bf16[64,4,256]{2,0,1:T(8,128)(2,1)}), bf16[64,4,256]{2,0,1:T(8,128)(2,1)S(1)}, u32[]{:S(2)}, u32[]{:S(2)}) async-start(bf16[64,4,256]{2,0,1:T(8,128)(2,1)} %bitcast.32), calls=%async_computation | async-start | bytes 262144 | tf_op jit(solution)/shard_map/all_to_all | solution.py:68
where the time goes:
time: 92.7 us; the launch traced here: 92.3 us
  blocking collectives  79.2 us (85%)
  other arithmetic  4.2 us (5%)
  starting transfers between devices  3.33 us (4%)
  local copies, waits for them, and re-layouts  2.52 us (3%)
  matrix products  2.32 us (3%)
    all_gather x1, blocking collectives, body(): gathered = lax.all_gather(hidden, 'vocab', axis=0, tiled=True)  32.5 us
    pmax x1, blocking collectives, body(): peak_value = lax.pmax(local_peak, 'vocab')  21.3 us
    psum x1, blocking collectives, body(): denominator, target_logit = lax.psum((local_total, local_target), 'vocab')  17.1 us
    all_gather x1, blocking collectives, body(): everyone = lax.all_gather(gathered, 'batch', axis=0, tiled=True)  8.24 us
    all_to_all x1, starting transfers between devices, body(): lax.all_to_all(grad_logits, 'batch', split_axis=1, concat_axis=0, tiled=T...  3.33 us
  transfers between devices with their start and end apart: 1, of which 0 were waited for; matrix products, arithmetic and copies ran while one was open for 1% of the time, Pallas kernels for 0%

commit v1 on v0

--- a/solution.py
+++ b/solution.py
@@ -66,7 +66,13 @@
         .reshape(token_count, local_rows)
     )
     columns = lax.all_to_all(grad_logits, "batch", split_axis=1, concat_axis=0, tiled=True)
-    everyone = lax.all_gather(gathered, "batch", axis=0, tiled=True)
+    size = lax.axis_size("batch")
+    current, blocks = (gathered, [gathered])
+    for _ in range(size - 1):
+        current = lax.ppermute(current, "batch", [(i, (i + 1) % size) for i in range(size)])
+        blocks.insert(0, current)
+    line = jnp.concatenate(blocks, axis=0)
+    everyone = jnp.roll(line, (lax.axis_index("batch") + 1) * gathered.shape[0], axis=0)
     summed = jnp.zeros((columns.shape[1], gathered.shape[1]), jnp.float32)
     for source in range(batch_count):
         slice_grad = columns[source * token_count : (source + 1) * token_count]

time: 92.7 us -> 99 us (1.068); the launches traced: 92.3 us -> 97.4 us
  blocking collectives: 79.2 us -> 71.1 us
  local copies, waits for them, and re-layouts: 2.52 us -> 7.8 us
  waiting for transfers between devices: 0.01 us -> 4.37 us
  matrix products: 2.32 us -> 5.95 us
    all_gather x1 -> x0, blocking collectives: 8.24 us -> none  [body(): everyone = lax.all_gather(gathered, 'batch', axis=0, tiled=True)]
    unnamed x2 -> x9, local copies, waits for them, and re-layouts: 0.01 us -> 4.61 us
    ppermute x0 -> x3, waiting for transfers between devices: none -> 4.37 us  [body(): lax.ppermute(current, 'batch', [(i, (i + 1) % size) for i in range(size)])]
    dot_general x4, matrix products: 1.25 us -> 4.88 us  [body(): lax.dot_general(slice_grad, slice_rows, (((0,), (0,)), ((), ())), preferr...]
  transfers between devices with their start and end apart: 1 -> 4, of which waited for: 0 -> 1; matrix products, arithmetic and copies ran while one was open for 1% -> 12% of each run, Pallas kernels for 0% -> 0%
where the time goes in v1:
time: 99 us; the launch traced here: 97.4 us
  blocking collectives  71.1 us (72%)
  local copies, waits for them, and re-layouts  7.8 us (8%)
  matrix products  5.95 us (6%)
  waiting for transfers between devices  4.37 us (4%)
  other arithmetic  4.05 us (4%)
  starting transfers between devices  3.38 us (3%)
    all_gather x1, blocking collectives, body(): gathered = lax.all_gather(hidden, 'vocab', axis=0, tiled=True)  32.7 us
    pmax x1, blocking collectives, body(): peak_value = lax.pmax(local_peak, 'vocab')  21.3 us
    psum x1, blocking collectives, body(): denominator, target_logit = lax.psum((local_total, local_target), 'vocab')  17.1 us
    dot_general x4, matrix products, body(): lax.dot_general(slice_grad, slice_rows, (((0,), (0,)), ((), ())), preferr...  4.88 us
    unnamed x9, local copies, waits for them, and re-layouts  4.61 us
    ppermute x3, waiting for transfers between devices, body(): lax.ppermute(current, 'batch', [(i, (i + 1) % size) for i in range(size)])  4.37 us
    all_to_all x1, starting transfers between devices, body(): lax.all_to_all(grad_logits, 'batch', split_axis=1, concat_axis=0, tiled=T...  3.33 us
  transfers between devices with their start and end apart: 4, of which 1 were waited for; matrix products, arithmetic and copies ran while one was open for 12% of the time, Pallas kernels for 0%

profile of v1, /device:TPU:0, one launch (start us, length us, event | category | flops | bytes accessed | tf_op | source)
XLA Modules:
  0.0 97.4 jit_solution(7140299390625155706)
XLA Ops:
  0.6 0.0 copy-start
  0.6 32.7 %all_gather.3 = bf16[64,1024]{1,0:T(8,128)(2,1)S(1)} all-gather(bf16[8,1024]{1,0:T(8,128)(2,1)} %param.6), channel_id=1, replica_groups=mesh['vocab'=8,'batch'=4] {'vocab'}, dimensions={0}, use_global_device_ids=true | all-gather | bytes 147456 | tf_op jit(solution)/shard_map/all_gather | solution.py:19
  33.3 0.0 collective-permute-start
  33.4 0.7 convert_log_fusion
  34.0 0.1 broadcast_bitcast_fusion
  34.1 0.1 iota_add_fusion
  34.2 0.1 add.106
  34.3 1.0 %compare_reduce_fusion = pred[200,8]{0,1:T(8,128)(4,1)S(1)} fusion(s32[200,64]{0,1:T(8,128)} %param.9, s32[8]{0:T(128)S(1)} %iota_add_fusion.1), kind=kLoop, calls=%fused_computation.7 | loop fusion | flops 203200 | bytes 52832 | tf_op jit(solution)/shard_map/reduce_or | solution.py:32
  35.3 0.7 select_reduce_fusion.1
  36.0 0.2 convolution_compare_fusion
  36.2 0.1 copy.13
  36.3 0.8 reshape.91
  37.1 0.1 eq.69
  37.2 0.1 broadcast_in_dim.53
  37.3 0.0 copy-done
  37.4 0.9 fusion.3
  38.2 21.3 %pmax.7 = f32[64]{0:T(128)S(1)} all-reduce(f32[64]{0:T(128)S(1)} %get-tuple-element.8), channel_id=1, replica_groups=mesh['vocab'=8,'batch'=4] {'vocab'}, use_global_device_ids=true, to_apply=%region_3.4 | all-reduce | flops 64 | bytes 512 | tf_op jit(solution)/shard_map/pmax | solution.py:54
  59.5 0.3 fusion
  59.8 17.1 %all-reduce = (f32[64]{0:T(128)S(1)}, f32[64]{0:T(128)S(1)}) all-reduce(f32[64]{0:T(128)S(1)} %get-tuple-element.3, f32[64]{0:T(128)S(1)} %get-tuple-element.2), channel_id=1, replica_groups=mesh['vocab'=8,'batch'=4] {'vocab'}, use_global_device_ids=true, to_apply=%region_5.6 | all-reduce | flops 128 | bytes 1024 | tf_op jit(solution)/shard_map/psum | solution.py:58
  76.9 0.0 collective-permute-done
  76.9 0.0 collective-permute-start.1
  77.0 4.4 %collective-permute-done.1 = bf16[64,1024]{1,0:T(8,128)(2,1)S(1)} collective-permute-done((bf16[64,1024]{1,0:T(8,128)(2,1)S(1)}, bf16[64,1024]{1,0:T(8,128)(2,1)S(1)}, u32[]{:S(2)}, u32[]{:S(2)}) %collective-permute-start.1) | collective-permute-done | bytes 131104 | tf_op jit(solution)/shard_map/ppermute | solution.py:72
  81.3 0.0 collective-permute-start.2
  81.3 0.1 fusion.2
  81.5 0.7 copy.21
  82.2 3.3 %all-to-all-start = ((bf16[64,4,256]{2,0,1:T(8,128)(2,1)}), bf16[64,4,256]{2,0,1:T(8,128)(2,1)S(1)}, u32[]{:S(2)}, u32[]{:S(2)}) async-start(bf16[64,4,256]{2,0,1:T(8,128)(2,1)} %bitcast.32), calls=%async_computation | async-start | bytes 262144 | tf_op jit(solution)/shard_map/all_to_all | solution.py:68
  85.5 0.6 dynamic_slice.12
  86.1 0.0 collective-permute-done.2
  86.1 0.6 constant_dynamic-update-slice_fusion.7
  86.7 0.7 constant_dynamic-update-slice_fusion.6
  87.4 0.7 constant_dynamic-update-slice_fusion.5
  88.1 0.7 constant_dynamic-update-slice_fusion.4
  88.7 0.7 constant_dynamic-update-slice_fusion.3
  89.4 0.6 constant_dynamic-update-slice_fusion.2
  90.0 0.7 constant_dynamic-update-slice_fusion.1
  90.7 0.7 constant_dynamic-update-slice_fusion
  91.4 0.0 all-to-all-done
  91.4 1.2 %convolution_convert_fusion.3 = bf16[256,1024]{1,0:T(8,128)(2,1)S(1)} fusion(bf16[512,1024]{1,0:T(8,128)(2,1)} %constant_dynamic-update-slice_fusion, s32[]{:T(128)S(6)} %select_n.61, bf16[4,64,256]{2,1,0:T(8,128)(2,1)S(1)} %bitcast.36), kind=kOutput, calls=%fused_computation.3 | convolution fusion | flops 33816576 | bytes 688132 | tf_op jit(solution)/shard_map/dot_general | solution.py:80
  92.6 1.2 %convolution_convert_fusion.1 = bf16[256,1024]{1,0:T(8,128)(2,1)S(1)} fusion(bf16[512,1024]{1,0:T(8,128)(2,1)} %constant_dynamic-update-slice_fusion, s32[]{:T(128)S(6)} %add.124, bf16[4,64,256]{2,1,0:T(8,128)(2,1)S(1)} %bitcast.37), kind=kOutput, calls=%fused_computation.1 | convolution fusion | flops 33816576 | bytes 688132 | tf_op jit(solution)/shard_map/dot_general | solution.py:80
  93.8 1.2 %convolution_convert_fusion.2 = bf16[256,1024]{1,0:T(8,128)(2,1)S(1)} fusion(bf16[512,1024]{1,0:T(8,128)(2,1)} %constant_dynamic-update-slice_fusion, s32[]{:T(128)S(6)} %add.123, bf16[4,64,256]{2,1,0:T(8,128)(2,1)S(1)} %bitcast.38), kind=kOutput, calls=%fused_computation.2 | convolution fusion | flops 33816576 | bytes 688132 | tf_op jit(solution)/shard_map/dot_general | solution.py:80
  95.1 1.2 %convolution_convert_fusion = bf16[256,1024]{1,0:T(8,128)(2,1)S(1)} fusion(bf16[512,1024]{1,0:T(8,128)(2,1)} %constant_dynamic-update-slice_fusion, s32[]{:T(128)S(6)} %add.125, bf16[4,64,256]{2,1,0:T(8,128)(2,1)S(1)} %bitcast.39), kind=kOutput, calls=%fused_computation | convolution fusion | flops 33816576 | bytes 688132 | tf_op jit(solution)/shard_map/dot_general | solution.py:80
  96.3 1.1 %add_convert_fusion = bf16[256,1024]{1,0:T(8,128)(2,1)} fusion(bf16[256,1024]{1,0:T(8,128)(2,1)S(1)} %convolution_convert_fusion, bf16[256,1024]{1,0:T(8,128)(2,1)S(1)} %convolution_convert_fusion.1, bf16[256,1024]{1,0:T(8,128)(2,1)S(1)} %convolution_convert_fusion.2, bf16[256,1024]{1,0:T(8,128)(2,1)S(1)} %convolution_convert_fusion.3), kind=kLoop, calls=%fused_computation.6 | loop fusion | flops 2097152 | bytes 2621440 | tf_op jit(solution)/shard_map/convert_element_type | solution.py:85
  (6 shorter events, 0.1 us)
Async XLA Ops:
  0.6 36.7 %copy-start = (bf16[1024,1024]{1,0:T(8,128)(2,1)S(1)}, bf16[1024,1024]{1,0:T(8,128)(2,1)}, u32[]{:S(2)}) copy-start(bf16[1024,1024]{1,0:T(8,128)(2,1)} %param.7) | copy-start | bytes 6291460
  33.3 43.6 %collective-permute-start = (bf16[64,1024]{1,0:T(8,128)(2,1)S(1)}, bf16[64,1024]{1,0:T(8,128)(2,1)S(1)}, u32[]{:S(2)}, u32[]{:S(2)}) collective-permute-start(bf16[64,1024]{1,0:T(8,128)(2,1)S(1)} %all_gather.3), channel_id=1, source_target_pairs={{0,1},{1,2},{2,3},{3,0},{4,5},{5,6},{6,7},{7,4},{8,9},{9,10},{10,1... | collective-permute-start | bytes 393224 | tf_op jit(solution)/shard_map/ppermute | solution.py:72
  76.9 4.4 %collective-permute-start.1 = (bf16[64,1024]{1,0:T(8,128)(2,1)S(1)}, bf16[64,1024]{1,0:T(8,128)(2,1)S(1)}, u32[]{:S(2)}, u32[]{:S(2)}) collective-permute-start(bf16[64,1024]{1,0:T(8,128)(2,1)S(1)} %collective-permute-done), channel_id=1, source_target_pairs={{0,1},{1,2},{2,3},{3,0},{4,5},{5,6},{6,7},{7,4},{8,9},{9,10},{10,1... | collective-permute-start | bytes 393224 | tf_op jit(solution)/shard_map/ppermute | solution.py:72
  81.3 4.8 %collective-permute-start.2 = (bf16[64,1024]{1,0:T(8,128)(2,1)S(1)}, bf16[64,1024]{1,0:T(8,128)(2,1)S(1)}, u32[]{:S(2)}, u32[]{:S(2)}) collective-permute-start(bf16[64,1024]{1,0:T(8,128)(2,1)S(1)} %collective-permute-done.1), channel_id=1, source_target_pairs={{0,1},{1,2},{2,3},{3,0},{4,5},{5,6},{6,7},{7,4},{8,9},{9,10},{10,1... | collective-permute-start | bytes 393224 | tf_op jit(solution)/shard_map/ppermute | solution.py:72
  82.2 9.2 %all-to-all-start = ((bf16[64,4,256]{2,0,1:T(8,128)(2,1)}), bf16[64,4,256]{2,0,1:T(8,128)(2,1)S(1)}, u32[]{:S(2)}, u32[]{:S(2)}) async-start(bf16[64,4,256]{2,0,1:T(8,128)(2,1)} %bitcast.32), calls=%async_computation | async-start | bytes 262144 | tf_op jit(solution)/shard_map/all_to_all | solution.py:68
